TPU v7x, 32 devices: a whole 2x2x4 slice. The times are simulated.
32 devices in a mesh: row: 8 (over z, x), col: 4 (over y, core).
Axes of the slice: x: 2, y: 2, z: 4, core: 2. Of those that a mesh axis runs over, the one named last changes fastest.
Arguments:
- near_blocks: bfloat16 [4096, 4096], P('row', 'col'), may hold values from -0.1875 to 0.1875
- pattern: int32 [8, 4], P('row', 'col'), may hold values 0 or 1
- iterate: bfloat16 [4096, 256], P('col'), may hold values from -6 to 6
- right_side: float32 [4096, 256], P(('row', 'col')), may hold values from -6 to 6
- basis: bfloat16 [4096, 512], P(('row', 'col')), may hold values from -0.1875 to 0.1875
- leaf_weight: float32 [4096], P(('row', 'col')), may hold values from 0.25 to 4
- transfers: bfloat16 [6, 512, 512], P(None, 'col'), may hold values from -0.1875 to 0.1875
- inverses: bfloat16 [7, 512, 512], P(None, 'col'), may hold values from -0.25 to 0.25
Outputs:
- correction: float32 [4096, 256], P(('row', 'col'))
Inputs may be any that keep to these rules, and one draw needn't show every extreme that they name: `pattern`: 0 or 1 for each pair of a row shard and a leaf column.
All inputs are finite; a program needn't handle non-finite values.
Results may differ from a plain program's by a relative error of at most 0.0003.
Values may be sent and summed in bfloat16 or wider, within the bound.
A program may use at most 64 MiB of HBM per device.

v0:
```python
import functools

import jax
import jax.numpy as jnp
from jax import lax
from jax.experimental import pallas as pl
from jax.experimental.pallas import tpu as pltpu
from jax.sharding import PartitionSpec as P

F32, BF16 = jnp.float32, jnp.bfloat16


def thin(x, mat, turned):
    n = x.shape[0]
    high = x.astype(BF16).astype(F32)
    both = jnp.concatenate([high, x - high], axis=0).astype(BF16)
    dims = (((1,), (1 if turned else 0,)), ((), ()))
    r = lax.dot_general(both, mat, dims, preferred_element_type=F32)
    return r[:n] + r[n:]


def split(ref, x):
    high = x.astype(BF16)
    ref[0] = high
    ref[1] = (x - high.astype(F32)).astype(BF16)


def pair_dot(lhs, rhs, dims):
    total = None
    for a in lhs:
        for b in rhs:
            r = lax.dot_general(a, b, (dims, ((), ())), preferred_element_type=F32)
            total = r if total is None else total + r
    return total


def counts(cols, levels):
    chips = cols
    mats = 2 * levels + 1
    swaps = levels + levels * (levels - 1) // 2
    remote = (
        4 * (cols // 2) - 1
        + 2 * cols - 1
        + mats * (2 * (cols // 2 - 1) + 1)
        + 1 + chips - 1
        + swaps
        + 2 * cols - 1
    )
    return chips, mats, swaps, remote


def kernel(
    cols, levels,
    near, pattern, iterate, right, basis, weight, transfers, inverses,
    out,
    near_v, iter_v, right_v, vfull, dfull, mats, part, corebuf, red, halfbuf,
    swap_out, swap_in, fin_out, fin_in, weighted, block, products, local_sem, send_sem, recv_sem,
):
    chips, n_mats, _, _ = counts(cols, levels)
    row, col = lax.axis_index("row"), lax.axis_index("col")
    leaf, half = row // 2, row % 2
    lane, core = col // 2, col % 2
    lanes = cols // 2
    chip = half * lanes + lane
    group = 2 * cols
    rhs = iterate.shape[1]
    n = rhs // group
    own_rows = basis.shape[0]
    mat_rows = transfers.shape[1]
    partner = (row, col + 1 - 2 * core)

    def chip_device(c, k):
        return (leaf * 2 + c // lanes, (c % lanes) * 2 + k)

    def place(c, k):
        return (c // lanes) * cols + (c % lanes) * 2 + k

    def rows_at(c, k, size):
        return pl.ds(pl.multiple_of(place(c, k) * size, size), size)

    def sibling(bit):
        b = (leaf // 2**bit) % 2
        return ((leaf + (1 - 2 * b) * 2**bit) * 2 + half, col)

    used = [0]
    started = []

    def send(src, dst, device):
        k = used[0]
        used[0] += 1
        copy = pltpu.make_async_remote_copy(
            src_ref=src, dst_ref=dst, send_sem=send_sem.at[k], recv_sem=recv_sem.at[k],
            device_id=device, device_id_type=pl.DeviceIdType.MESH,
        )
        copy.start()
        started.append(copy)
        return copy

    locals_used = [0]

    def local(src, dst):
        k = locals_used[0]
        locals_used[0] += 1
        copy = pltpu.make_async_copy(src, dst, local_sem.at[k])
        copy.start()
        return copy

    offsets = [(1, d) for d in range(1, lanes)] + [(1, 0)] + [(0, d) for d in range(1, lanes)]

    def ahead(o):
        return ((half + o[0]) % 2) * lanes + (lane + o[1]) % lanes

    def behind(o):
        return ((half + o[0]) % 2) * lanes + (lane + lanes - o[1]) % lanes

    barrier = pltpu.get_barrier_semaphore()
    others = []
    for d in range(chips):
        c = (chip + d) % chips
        if d > 0:
            others.append(chip_device(c, core))
        others.append(chip_device(c, 1 - core))
    others += [sibling(b) for b in range(levels)]
    for device in others:
        pl.semaphore_signal(
            barrier, inc=1, device_id=device, device_id_type=pl.DeviceIdType.MESH
        )
    mine = rows_at(chip, core, own_rows)
    near_copy = local(near, near_v)
    iter_copy = local(iterate, iter_v)
    mine_in_half = pl.ds(pl.multiple_of(col * own_rows, own_rows), own_rows)
    aligned = own_rows % 128 == 0
    if not aligned:
        right_v[...] = jnp.zeros_like(right_v)
    right_copy = local(right, right_v if aligned else right_v.at[mine_in_half])
    base_copy = local(basis, vfull.at[mine])
    weight_copy = local(weight, dfull.at[place(chip, core)])

    def source(m):
        k = m if m < levels else m - levels
        index = 2 * cols - (2 * cols // 2**k) + leaf // 2**k
        return (transfers if m < levels else inverses).at[index]

    order = list(range(levels)) + [levels + k for k in range(levels, -1, -1)]
    own_mat = pl.ds(pl.multiple_of(col * mat_rows, mat_rows), mat_rows)
    mat_local = {m: local(source(m), mats.at[m, own_mat]) for m in order}

    pl.semaphore_wait(barrier, len(others))

    across = ((leaf * 2 + 1 - half), col)
    base_lane = [
        send(basis, vfull.at[mine], (row, ((lane + d) % lanes) * 2 + core))
        for d in range(1, lanes)
    ]
    base_across = send(basis, vfull.at[mine], across)
    base_partner = send(basis, vfull.at[mine], partner)

    def base_slot(h, d):
        return vfull.at[rows_at(h * lanes + (lane + lanes - d) % lanes, core, own_rows)]

    weight_sends = []
    for d in range(chips):
        c = (chip + d) % chips
        for k in ([core, 1 - core] if d > 0 else [1 - core]):
            weight_sends.append(
                send(weight, dfull.at[place(chip, core)], chip_device(c, k))
            )
    mat_far, mat_near, mat_forward = {}, {}, {}

    def start_mat(m):
        mat_far[m] = [
            send(source(m), mats.at[m, own_mat], (row, ((lane + d) % lanes) * 2 + core))
            for d in range(1, lanes)
        ]
        mat_near[m] = send(source(m), mats.at[m, own_mat], partner)

    def forward_mat(m):
        mat_forward[m] = []
        for d in range(1, lanes):
            mat_far[m][d - 1].wait_recv()
            came = ((lane + lanes - d) % lanes) * 2 + core
            slot = mats.at[m, pl.ds(pl.multiple_of(came * mat_rows, mat_rows), mat_rows)]
            mat_forward[m].append(send(slot, slot, partner))

    def finish_mat(m):
        mat_local[m].wait()
        mat_near[m].wait_recv()
        for copy in mat_forward[m]:
            copy.wait_recv()

    start_mat(order[0])

    near_copy.wait()
    iter_copy.wait()
    right_copy.wait()
    present = pattern[0, 0].astype(F32)
    turned = lax.dot_general(
        iter_v[...], near_v[...], (((0,), (1,)), ((), ())), preferred_element_type=F32
    )
    if aligned:
        part[...] = -present * turned
        part[:, mine_in_half] = part[:, mine_in_half] + right_v[...].T
    else:
        part[...] = right_v[...].T - present * turned

    wide = rhs // 2
    core_send = send(
        part.at[pl.ds(pl.multiple_of((1 - core) * wide, wide), wide)], corebuf, partner
    )
    core_send.wait_recv()
    base_forward = []
    for d in range(1, lanes):
        base_lane[d - 1].wait_recv()
        base_forward.append(send(base_slot(half, d), base_slot(half, d), partner))
    applied = part[pl.ds(pl.multiple_of(core * wide, wide), wide), :] + corebuf[...]
    base_copy.wait()
    base_partner.wait_recv()
    for copy in base_forward:
        copy.wait_recv()
    half_rows = near.shape[0]
    half_base = vfull[pl.ds(pl.multiple_of(half * half_rows, half_rows), half_rows), :]
    red[...] = thin(applied, half_base, False)
    half_sends = []
    for o in offsets:
        c = ahead(o)
        half_sends.append(
            send(
                red.at[pl.ds(pl.multiple_of(c * n, n), n)],
                halfbuf.at[chip],
                chip_device(c, core),
            )
        )
    relays = [send(base_slot(half, d), base_slot(half, d), across) for d in range(1, lanes)]
    for m in order[1:]:
        start_mat(m)
    base_across.wait_recv()
    far_forward = [send(base_slot(1 - half, 0), base_slot(1 - half, 0), partner)]

    def forward_relays():
        for d in range(1, lanes):
            relays[d - 1].wait_recv()
            far_forward.append(send(base_slot(1 - half, d), base_slot(1 - half, d), partner))

    forward_mat(order[0])
    gathered = red[pl.ds(pl.multiple_of(chip * n, n), n), :]
    for o, copy in zip(offsets, half_sends):
        copy.wait_recv()
        gathered = gathered + halfbuf[behind(o)]
    swaps_used = [0]

    def swap_sum(x, bit, meanwhile=(), then=None):
        k = swaps_used[0]
        swaps_used[0] += 1
        swap_out[k] = x
        copy = send(swap_out.at[k], swap_in.at[k], sibling(bit))
        for m in meanwhile:
            forward_mat(m)
        if then is not None:
            then()
        copy.wait_recv()
        return x + swap_in[k]

    def form_leaf():
        weight_copy.wait()
        for copy in far_forward:
            copy.wait_recv()
        for copy in weight_sends:
            copy.wait_recv()
        weights = jnp.concatenate([dfull[p] for p in range(group)], axis=0).T
        for p in range(group):
            rows = pl.ds(p * own_rows, own_rows)
            scaled = weights[:, p:p + 1] * vfull[rows, :].astype(F32)
            high = scaled.astype(BF16)
            weighted[0, rows, :] = high
            weighted[1, rows, :] = (scaled - high.astype(F32)).astype(BF16)
        split(block, pair_dot([vfull[...]], [weighted[0], weighted[1]], ((0,), (0,))))

    def form_products():
        split(products.at[0], pair_dot([block[0], block[1]], [mats[0]], ((1,), (0,))))

    projected = [gathered]
    pending = order[1:]
    for k in range(levels):
        finish_mat(k)
        lifted = thin(projected[k], mats[k], False)
        now, pending = pending[:1], pending[1:]
        if k < levels - 1:
            projected.append(swap_sum(lifted, k, now, forward_relays if k == 0 else None))
        else:
            projected.append(swap_sum(lifted, k, now, form_leaf))
    finish_mat(2 * levels)
    correction = thin(projected[levels], mats[2 * levels], True)
    for k in range(levels - 1, -1, -1):
        if k == 0:
            s = thin(correction, products[0, 0], True) + thin(correction, products[0, 1], True)
        else:
            y = correction
            for j in range(k, -1, -1):
                y = thin(y, mats[j], True)
            s = thin(y, block[0], True) + thin(y, block[1], True)
        for j in range(k):
            s = thin(s, mats[j], False)
            s = swap_sum(s, j, pending[:1], form_products if k == 1 else None)
            pending = pending[1:]
        for m in pending[:1] if levels + k in pending else ():
            forward_mat(m)
            pending = pending[1:]
        finish_mat(levels + k)
        correction = thin(projected[k] - s, mats[levels + k], True)
    rows = thin(correction, vfull[...], True)
    for p in range(group):
        fin_out[p] = rows[:, p * own_rows:(p + 1) * own_rows]
    first = (core * chips + chip) * n
    slot = pl.ds(pl.multiple_of(first, n), n)
    fin_sends = []
    for o in offsets + [(0, 0)]:
        c = ahead(o)
        for k in ([core, 1 - core] if o != (0, 0) else [1 - core]):
            fin_sends.append(send(fin_out.at[place(c, k)], fin_in.at[slot], chip_device(c, k)))
    fin_in[slot, :] = fin_out[place(chip, core)]
    for copy in fin_sends:
        copy.wait_recv()
    out[...] = fin_in[...]
    for copy in started:
        copy.wait_send()


def on_device(near_blocks, pattern, iterate, right_side, basis, leaf_weight, transfers, inverses):
    cols = lax.axis_size("col")
    levels = cols.bit_length() - 1
    chips, n_mats, swaps, remote = counts(cols, levels)
    group = 2 * cols
    rank = basis.shape[1]
    own_rows = basis.shape[0]
    rhs = iterate.shape[1]
    n = rhs // group
    half_rows = near_blocks.shape[0]
    any_spec = pl.BlockSpec(memory_space=pl.ANY)
    turned = pl.pallas_call(
        functools.partial(kernel, cols, levels),
        out_shape=jax.ShapeDtypeStruct((rhs, own_rows), F32),
        in_specs=[any_spec, pl.BlockSpec(memory_space=pltpu.SMEM)] + [any_spec] * 6,
        out_specs=pl.BlockSpec(memory_space=pltpu.VMEM),
        scratch_shapes=[
            pltpu.VMEM(near_blocks.shape, BF16),
            pltpu.VMEM(iterate.shape, BF16),
            pltpu.VMEM((own_rows if own_rows % 128 == 0 else half_rows, rhs), F32),
            pltpu.VMEM((2 * half_rows, rank), BF16),
            pltpu.VMEM((group, 1, own_rows), F32),
            pltpu.VMEM((n_mats, rank, rank), BF16),
            pltpu.VMEM((rhs, half_rows), F32),
            pltpu.VMEM((rhs // 2, half_rows), F32),
            pltpu.VMEM((rhs // 2, rank), F32),
            pltpu.VMEM((chips, n, rank), F32),
            pltpu.VMEM((swaps, n, rank), F32),
            pltpu.VMEM((swaps, n, rank), F32),
            pltpu.VMEM((group, n, own_rows), F32),
            pltpu.VMEM((rhs, own_rows), F32),
            pltpu.VMEM((2, 2 * half_rows, rank), BF16),
            pltpu.VMEM((2, rank, rank), BF16),
            pltpu.VMEM((levels, 2, rank, rank), BF16),
            pltpu.SemaphoreType.DMA((5 + n_mats,)),
            pltpu.SemaphoreType.DMA((remote,)),
            pltpu.SemaphoreType.DMA((remote,)),
        ],
        compiler_params=pltpu.CompilerParams(collective_id=0, has_side_effects=True),
    )(
        near_blocks, pattern, iterate, right_side, basis,
        leaf_weight.reshape(1, own_rows), transfers, inverses,
    )
    return turned.T


def solution(mesh):
    placed = (
        P("row", "col"),
        P("row", "col"),
        P("col", None),
        P(("row", "col"), None),
        P(("row", "col"), None),
        P(("row", "col")),
        P(None, "col", None),
        P(None, "col", None),
    )
    return jax.shard_map(
        on_device, mesh=mesh, in_specs=placed, out_specs=P(("row", "col"), None), check_vma=False
    )
```

profile of v0, /device:TPU:0, one launch (start us, length us, event | category | flops | bytes accessed | tf_op | source)
XLA Modules:
  0.0 38.7 jit_solution(8853460789073847435)
XLA Ops:
  0.7 36.4 %shard_map.82 = f32[256,128]{1,0:T(8,128)} custom-call(bf16[512,1024]{1,0:T(8,128)(2,1)} %near.1, s32[1,1]{1,0:T(1,128)S(6)} %copy.10.pattern, bf16[1024,256]{1,0:T(8,128)(2,1)} %iterate.1, f32[128,256]{1,0:T(8,128)} %right.1, bf16[128,512]{1,0:T(8,128)(2,1)} %basis.1, f32[1,128]{1,0:T(1,128)} %bitcast.3, bf16[6,128,512]{2,1,0:T(8,128)(2,1)} %transfers.1, ...), custom_call_target="tpu_custom_call" | custom-call | tf_op jit(solution)/shard_map/pallas_call | solution.py:339
  37.0 1.7 %copy.9 = f32[128,256]{1,0:T(8,128)} copy(f32[128,256]{0,1:T(8,128)} %bitcast.2) | data formatting | bytes 262144 | tf_op jit(solution)/shard_map/transpose | solution.py:371
where the time goes:
time: 38.9 us; the launch traced here: 38.7 us
  Pallas kernels  36.4 us (94%)
  local copies, waits for them, and re-layouts  1.66 us (4%)
  between operations  0.66 us (2%)
    pallas_call x1, Pallas kernels, on_device(): pl.pallas_call(functools.partial(kernel, cols, levels), out_shape=jax.Sha...  36.4 us
    transpose x1, local copies, waits for them, and re-layouts, on_device(): return turned.T  1.66 us

commit v1 on v0

--- a/solution.py
+++ b/solution.py
@@ -338,7 +338,7 @@
     any_spec = pl.BlockSpec(memory_space=pl.ANY)
     turned = pl.pallas_call(
         functools.partial(kernel, cols, levels),
-        out_shape=jax.ShapeDtypeStruct((rhs, own_rows), F32),
+        out_shape=pltpu.VMEM((rhs, own_rows), F32),
         in_specs=[any_spec, pl.BlockSpec(memory_space=pltpu.SMEM)] + [any_spec] * 6,
         out_specs=pl.BlockSpec(memory_space=pltpu.VMEM),
         scratch_shapes=[

time: 38.9 us -> 37.3 us (0.959)
  local copies, waits for them, and re-layouts: 1.66 us -> 0.76 us
  Pallas kernels: 36.4 us -> 35.7 us
    transpose x1, local copies, waits for them, and re-layouts: 1.66 us -> 0.76 us  [on_device(): return turned.T]
    pallas_call x1, Pallas kernels: 36.4 us -> 35.7 us  [on_device(): pl.pallas_call(functools.partial(kernel, cols, levels), out_shape=pltpu.V...]
where the time goes in v1:
time: 37.3 us; the launch traced here: 37.2 us
  Pallas kernels  35.7 us (96%)
  local copies, waits for them, and re-layouts  0.76 us (2%)
  between operations  0.66 us (2%)
    pallas_call x1, Pallas kernels, on_device(): pl.pallas_call(functools.partial(kernel, cols, levels), out_shape=pltpu.V...  35.7 us
    transpose x1, local copies, waits for them, and re-layouts, on_device(): return turned.T  0.76 us

profile of v1, /device:TPU:0, one launch (start us, length us, event | category | flops | bytes accessed | tf_op | source)
XLA Modules:
  0.0 37.2 jit_solution(9022801624360810273)
XLA Ops:
  0.7 35.7 %shard_map.82 = f32[256,128]{1,0:T(8,128)S(1)} custom-call(bf16[512,1024]{1,0:T(8,128)(2,1)} %near.1, s32[1,1]{1,0:T(1,128)S(6)} %copy.10.pattern, bf16[1024,256]{1,0:T(8,128)(2,1)} %iterate.1, f32[128,256]{1,0:T(8,128)} %right.1, bf16[128,512]{1,0:T(8,128)(2,1)} %basis.1, f32[1,128]{1,0:T(1,128)} %bitcast.3, bf16[6,128,512]{2,1,0:T(8,128)(2,1)} %transfers.1, ...), custom_call_target="tpu_custom_call" | custom-call | tf_op jit(solution)/shard_map/pallas_call | solution.py:339
  36.4 0.8 %copy.9 = f32[128,256]{1,0:T(8,128)} copy(f32[128,256]{0,1:T(8,128)S(1)} %bitcast.2) | data formatting | bytes 262144 | tf_op jit(solution)/shard_map/transpose | solution.py:371

commit v2 on v1

--- a/solution.py
+++ b/solution.py
@@ -307,16 +307,21 @@
             pending = pending[1:]
         finish_mat(levels + k)
         correction = thin(projected[k] - s, mats[levels + k], True)
-    rows = thin(correction, vfull[...], True)
-    for p in range(group):
-        fin_out[p] = rows[:, p * own_rows:(p + 1) * own_rows]
     first = (core * chips + chip) * n
     slot = pl.ds(pl.multiple_of(first, n), n)
     fin_sends = []
-    for o in offsets + [(0, 0)]:
-        c = ahead(o)
-        for k in ([core, 1 - core] if o != (0, 0) else [1 - core]):
-            fin_sends.append(send(fin_out.at[place(c, k)], fin_in.at[slot], chip_device(c, k)))
+    for step in (1, 0):
+        side = (half + step) % 2
+        base = vfull[pl.ds(pl.multiple_of(side * half_rows, half_rows), half_rows), :]
+        rows = thin(correction, base, True)
+        for p in range(cols):
+            fin_out[side * cols + p] = rows[:, p * own_rows:(p + 1) * own_rows]
+        for o in [o for o in offsets if o[0] == step] + ([(0, 0)] if step == 0 else []):
+            c = ahead(o)
+            for k in ([core, 1 - core] if o != (0, 0) else [1 - core]):
+                fin_sends.append(
+                    send(fin_out.at[place(c, k)], fin_in.at[slot], chip_device(c, k))
+                )
     fin_in[slot, :] = fin_out[place(chip, core)]
     for copy in fin_sends:
         copy.wait_recv()

time: 37.3 us -> 37.4 us (level)
  no operation moved by 1% of the time
where the time goes in v2:
time: 37.4 us; the launch traced here: 37.3 us
  Pallas kernels  35.9 us (96%)
  local copies, waits for them, and re-layouts  0.76 us (2%)
  between operations  0.66 us (2%)
    pallas_call x1, Pallas kernels, on_device(): pl.pallas_call(functools.partial(kernel, cols, levels), out_shape=pltpu.V...  35.9 us
    transpose x1, local copies, waits for them, and re-layouts, on_device(): return turned.T  0.76 us

profile of v2, /device:TPU:0, one launch (start us, length us, event | category | flops | bytes accessed | tf_op | source)
XLA Modules:
  0.0 37.3 jit_solution(13731717935949141739)
XLA Ops:
  0.7 35.9 %shard_map.82 = f32[256,128]{1,0:T(8,128)S(1)} custom-call(bf16[512,1024]{1,0:T(8,128)(2,1)} %near.1, s32[1,1]{1,0:T(1,128)S(6)} %copy.10.pattern, bf16[1024,256]{1,0:T(8,128)(2,1)} %iterate.1, f32[128,256]{1,0:T(8,128)} %right.1, bf16[128,512]{1,0:T(8,128)(2,1)} %basis.1, f32[1,128]{1,0:T(1,128)} %bitcast.3, bf16[6,128,512]{2,1,0:T(8,128)(2,1)} %transfers.1, ...), custom_call_target="tpu_custom_call" | custom-call | tf_op jit(solution)/shard_map/pallas_call | solution.py:344
  36.5 0.8 %copy.9 = f32[128,256]{1,0:T(8,128)} copy(f32[128,256]{0,1:T(8,128)S(1)} %bitcast.2) | data formatting | bytes 262144 | tf_op jit(solution)/shard_map/transpose | solution.py:376
